TPU v7x, 32 devices: a whole 2x2x4 slice. The times are simulated.
32 devices in a mesh: dp: 16 (over z, y, core), tensor: 2 (over x).
Axes of the slice: x: 2, y: 2, z: 4, core: 2. Of those that a mesh axis runs over, the one named last changes fastest.
Arguments:
- frames_in: bfloat16 [2, 16, 1024, 1024], P(None, 'dp', 'tensor'), may hold values from -6 to 6
- phone_len: int32 [2, 16], P(None, 'dp'), may hold values from 10 to 204
- frame_len: int32 [2, 16], P(None, 'dp'), may hold values from 512 to 819
- section: int32 [2, 16], P(None, 'dp'), may hold values from 0 to 6
- norm_gain: float32 [2, 1024], replicated, may hold values from 0.5 to 1.5
- norm_bias: float32 [2, 1024], replicated, may hold values from -4 to 4
- ada_scale: float32 [2, 7, 1024], replicated, may hold values from 0.5 to 1.5
- ada_shift: float32 [2, 7, 1024], replicated, may hold values from -4 to 4
- w_qkv: bfloat16 [2, 1024, 3, 1024], P(None, None, None, 'tensor'), may hold values from -0.1875 to 0.1875
- w_out: bfloat16 [2, 1024, 1024], P(None, 'tensor'), may hold values from -4 to 4
- w_up: bfloat16 [2, 1024, 4096], P(None, None, 'tensor'), may hold values from -0.1875 to 0.1875
- w_down: bfloat16 [2, 4096, 1024], P(None, 'tensor'), may hold values from -0.09375 to 0.09375
- out_grad: bfloat16 [2, 16, 1024, 1024], P(None, 'dp', 'tensor'), may hold values from -6 to 6
Outputs:
- frames_out: float32 [2, 16, 1024, 1024], P(None, 'dp', 'tensor')
- frames_grad: float32 [2, 16, 1024, 1024], P(None, 'dp', 'tensor')
- grad_qkv: float32 [2, 1024, 3, 1024], P(None, None, None, 'tensor')
- grad_out: float32 [2, 1024, 1024], P(None, 'tensor')
- grad_up: float32 [2, 1024, 4096], P(None, None, 'tensor')
- grad_down: float32 [2, 4096, 1024], P(None, 'tensor')
- grad_norm_gain: float32 [2, 1024], replicated
- grad_norm_bias: float32 [2, 1024], replicated
- grad_ada_scale: float32 [2, 7, 1024], replicated
- grad_ada_shift: float32 [2, 7, 1024], replicated
All inputs are finite; a program needn't handle non-finite values.
Results may differ from a plain program's by a relative error of at most 0.028.
Values may be sent and summed in bfloat16 or wider, within the bound.
No kernel may reach another device: no remote copies, remote signals or barrier semaphores. Data moves between devices by JAX's collectives and lax.ppermute only.
A program may use at most 384 MiB of HBM per device.

v0:
```python
from functools import partial
import jax
import jax.numpy as jnp
from jax import lax
from jax.sharding import PartitionSpec as P

HEAD_DIM = 64
norm_eps = 1e-05
masked_score = -1000000000.0
contract_rows = (((0,), (0,)), ((), ()))
contract_cols = (((1,), (1,)), ((), ()))


def plain_norm(inputs):
    centered = inputs - jnp.mean(inputs, axis=-1, keepdims=True)
    variance = jnp.mean(centered * centered, axis=-1, keepdims=True)
    return centered * lax.rsqrt(variance + norm_eps)


def fixed_norm(inputs, gain_row, shift_row):
    return plain_norm(inputs) * gain_row + shift_row


def section_norm(inputs, scale_table, shift_table, picker):
    scale_row = jnp.dot(
        picker, scale_table, precision=lax.Precision.HIGHEST, preferred_element_type=jnp.float32
    )
    shift_row = jnp.dot(
        picker, shift_table, precision=lax.Precision.HIGHEST, preferred_element_type=jnp.float32
    )
    return plain_norm(inputs) * scale_row + shift_row


def gather_normed(normed_low):
    return lax.all_gather(normed_low, "tensor", axis=0, tiled=True)


def gather_again(normed_low):
    return lax.all_gather(normed_low, "tensor", axis=0, tiled=True)


def sum_branch(branch_part):
    return lax.psum_scatter(
        branch_part.astype(jnp.bfloat16), "tensor", scatter_dimension=0, tiled=True
    ).astype(jnp.float32)


def gather_grad(grad_low):
    return lax.all_gather(grad_low, "tensor", axis=0, tiled=True)


def sum_normed(grad_part):
    return lax.psum_scatter(
        grad_part.astype(jnp.bfloat16), "tensor", scatter_dimension=0, tiled=True
    ).astype(jnp.float32)


def key_allowed(query_pos, key_pos, prefix, valid_count, causal):
    allowed = key_pos[None, :] < valid_count
    if causal:
        allowed = allowed & ((key_pos[None, :] < prefix) | (key_pos[None, :] <= query_pos[:, None]))
    return allowed


def split_heads(projected):
    length = projected.shape[0]
    head_width = projected.shape[1] // 3
    head_count = head_width // HEAD_DIM
    query_rows = projected[:, :head_width].reshape(length, head_count, HEAD_DIM)
    key_rows = projected[:, head_width : 2 * head_width].reshape(length, head_count, HEAD_DIM)
    value_rows = projected[:, 2 * head_width :].reshape(length, head_count, HEAD_DIM)
    return (query_rows, key_rows, value_rows)


def block_scores(query_block, key_rows, block_start, prefix, valid_count, causal):
    block_rows = query_block.shape[0]
    length = key_rows.shape[0]
    scores = jnp.einsum(
        "qhd,khd->hqk", query_block, key_rows, preferred_element_type=jnp.float32
    ) * HEAD_DIM ** (-0.5)
    query_pos = block_start + lax.iota(jnp.int32, block_rows)
    key_pos = lax.iota(jnp.int32, length)
    allowed = key_allowed(query_pos, key_pos, prefix, valid_count, causal)
    return jnp.where(allowed[None], scores, masked_score)


def attend_forward(projected, prefix, valid_count, causal, block_rows):
    length = projected.shape[0]
    head_width = projected.shape[1] // 3
    query_rows, key_rows, value_rows = split_heads(projected)

    def one_block(block_start):
        query_block = lax.dynamic_slice_in_dim(query_rows, block_start, block_rows, 0)
        scores = block_scores(query_block, key_rows, block_start, prefix, valid_count, causal)
        highest = jnp.max(scores, axis=-1, keepdims=True)
        row_total = jnp.sum(jnp.exp(scores - highest), axis=-1, keepdims=True)
        log_total = highest + jnp.log(row_total)
        shares = jnp.exp(scores - log_total).astype(jnp.bfloat16)
        mixture = jnp.einsum("hqk,khd->qhd", shares, value_rows, preferred_element_type=jnp.float32)
        return (mixture.astype(jnp.bfloat16), log_total)

    starts = lax.iota(jnp.int32, length // block_rows) * block_rows
    mixture, log_totals = lax.map(one_block, starts)
    return (mixture.reshape(length, head_width), log_totals)


def attend_backward(projected, log_totals, grad_mixture, prefix, valid_count, causal, block_rows):
    length = projected.shape[0]
    head_width = projected.shape[1] // 3
    query_rows, key_rows, value_rows = split_heads(projected)
    grad_rows = grad_mixture.reshape(query_rows.shape)
    score_scale = HEAD_DIM ** (-0.5)

    def one_block(grad_state, block_item):
        block_start, log_total = block_item
        grad_key, grad_value = grad_state
        query_block = lax.dynamic_slice_in_dim(query_rows, block_start, block_rows, 0)
        grad_block = lax.dynamic_slice_in_dim(grad_rows, block_start, block_rows, 0)
        scores = block_scores(query_block, key_rows, block_start, prefix, valid_count, causal)
        shares = jnp.exp(scores - log_total)
        shares_low = shares.astype(jnp.bfloat16)
        grad_shares = jnp.einsum(
            "qhd,khd->hqk", grad_block, value_rows, preferred_element_type=jnp.float32
        )
        inner_sum = jnp.sum(shares * grad_shares, axis=-1, keepdims=True)
        grad_scores = (shares * (grad_shares - inner_sum)).astype(jnp.bfloat16)
        grad_query = (
            jnp.einsum("hqk,khd->qhd", grad_scores, key_rows, preferred_element_type=jnp.float32)
            * score_scale
        )
        grad_key = (
            grad_key
            + jnp.einsum(
                "hqk,qhd->khd", grad_scores, query_block, preferred_element_type=jnp.float32
            )
            * score_scale
        )
        grad_value = grad_value + jnp.einsum(
            "hqk,qhd->khd", shares_low, grad_block, preferred_element_type=jnp.float32
        )
        return ((grad_key, grad_value), grad_query)

    starts = lax.iota(jnp.int32, length // block_rows) * block_rows
    zero_rows = jnp.zeros(query_rows.shape, jnp.float32)
    grad_state, grad_query = lax.scan(one_block, (zero_rows, zero_rows), (starts, log_totals))
    grad_key, grad_value = grad_state
    joined = jnp.concatenate(
        [
            grad_query.reshape(length, head_width),
            grad_key.reshape(length, head_width),
            grad_value.reshape(length, head_width),
        ],
        axis=1,
    )
    return joined.astype(jnp.bfloat16)


def per_device(
    frames_in,
    phone_len,
    frame_len,
    section,
    norm_gain,
    norm_bias,
    ada_scale,
    ada_shift,
    w_qkv,
    w_out,
    w_up,
    w_down,
    out_grad,
):
    micro_count, local_seqs, local_rows, model_width = frames_in.shape
    seq_length = local_rows * lax.axis_size("tensor")
    block_rows = min(512, seq_length)
    section_count = ada_scale.shape[1]
    qkv_mats = [w_qkv[layer_index].reshape(model_width, -1) for layer_index in range(2)]
    acc_qkv = [jnp.zeros(qkv_mats[layer_index].shape, jnp.float32) for layer_index in range(2)]
    acc_out = [jnp.zeros(w_out.shape[1:], jnp.float32) for layer_index in range(2)]
    acc_up = [jnp.zeros(w_up.shape[1:], jnp.float32) for layer_index in range(2)]
    acc_down = [jnp.zeros(w_down.shape[1:], jnp.float32) for layer_index in range(2)]
    acc_gain = [jnp.zeros((model_width,), jnp.float32) for part_index in range(2)]
    acc_bias = [jnp.zeros((model_width,), jnp.float32) for part_index in range(2)]
    acc_scale = [jnp.zeros((section_count, model_width), jnp.float32) for part_index in range(2)]
    acc_shift = [jnp.zeros((section_count, model_width), jnp.float32) for part_index in range(2)]
    frames_list = []
    grads_list = []
    for micro_index in range(micro_count):
        prefix = phone_len[micro_index, 0]
        valid_count = prefix + frame_len[micro_index, 0]
        picker = (lax.iota(jnp.int32, section_count) == section[micro_index, 0]).astype(
            jnp.float32
        )[None, :]
        residual = frames_in[micro_index, 0].astype(jnp.float32)
        stored = []
        for layer_index in range(2):
            for part_index in range(2):
                if layer_index == 0:
                    normed, norm_back = jax.vjp(
                        fixed_norm, residual, norm_gain[part_index], norm_bias[part_index]
                    )
                else:
                    normed, norm_back = jax.vjp(
                        partial(section_norm, picker=picker),
                        residual,
                        ada_scale[part_index],
                        ada_shift[part_index],
                    )
                normed_low = normed.astype(jnp.bfloat16)
                gathered = gather_normed(normed_low)
                if part_index == 0:
                    projected = jnp.dot(
                        gathered, qkv_mats[layer_index], preferred_element_type=jnp.float32
                    ).astype(jnp.bfloat16)
                    mixture, log_totals = attend_forward(
                        projected, prefix, valid_count, layer_index == 0, block_rows
                    )
                    branch = sum_branch(
                        jnp.dot(mixture, w_out[layer_index], preferred_element_type=jnp.float32)
                    )
                    saved_state = (projected, log_totals, mixture)
                else:
                    hidden = jnp.dot(
                        gathered, w_up[layer_index], preferred_element_type=jnp.float32
                    )
                    active = jax.nn.gelu(hidden, approximate=True).astype(jnp.bfloat16)
                    branch = sum_branch(
                        jnp.dot(active, w_down[layer_index], preferred_element_type=jnp.float32)
                    )
                    saved_state = (hidden, active)
                kept_rows = normed_low
                stored.append((norm_back, kept_rows, saved_state))
                residual = residual + branch
        out_group = [residual]
        grad_rows = out_grad[micro_index, 0].astype(jnp.float32)
        for layer_index in (1, 0):
            for part_index in (1, 0):
                norm_back, kept_rows, saved_state = stored[2 * layer_index + part_index]
                gathered = gather_again(kept_rows)
                grad_whole = gather_grad(grad_rows.astype(jnp.bfloat16))
                if part_index == 1:
                    hidden, active = saved_state
                    acc_down[layer_index] = acc_down[layer_index] + lax.dot_general(
                        active, grad_whole, contract_rows, preferred_element_type=jnp.float32
                    )
                    grad_active = lax.dot_general(
                        grad_whole,
                        w_down[layer_index],
                        contract_cols,
                        preferred_element_type=jnp.float32,
                    )
                    gelu_value, gelu_back = jax.vjp(partial(jax.nn.gelu, approximate=True), hidden)
                    grad_hidden = gelu_back(grad_active)[0].astype(jnp.bfloat16)
                    acc_up[layer_index] = acc_up[layer_index] + lax.dot_general(
                        gathered, grad_hidden, contract_rows, preferred_element_type=jnp.float32
                    )
                    grad_normed = sum_normed(
                        lax.dot_general(
                            grad_hidden,
                            w_up[layer_index],
                            contract_cols,
                            preferred_element_type=jnp.float32,
                        )
                    )
                else:
                    projected, log_totals, mixture = saved_state
                    acc_out[layer_index] = acc_out[layer_index] + lax.dot_general(
                        mixture, grad_whole, contract_rows, preferred_element_type=jnp.float32
                    )
                    grad_mixture = lax.dot_general(
                        grad_whole,
                        w_out[layer_index],
                        contract_cols,
                        preferred_element_type=jnp.float32,
                    ).astype(jnp.bfloat16)
                    grad_projected = attend_backward(
                        projected,
                        log_totals,
                        grad_mixture,
                        prefix,
                        valid_count,
                        layer_index == 0,
                        block_rows,
                    )
                    acc_qkv[layer_index] = acc_qkv[layer_index] + lax.dot_general(
                        gathered, grad_projected, contract_rows, preferred_element_type=jnp.float32
                    )
                    grad_normed = sum_normed(
                        lax.dot_general(
                            grad_projected,
                            qkv_mats[layer_index],
                            contract_cols,
                            preferred_element_type=jnp.float32,
                        )
                    )
                grad_input, grad_first, grad_second = norm_back(grad_normed)
                grad_rows = grad_rows + grad_input
                if layer_index == 0:
                    acc_gain[part_index] = acc_gain[part_index] + grad_first
                    acc_bias[part_index] = acc_bias[part_index] + grad_second
                else:
                    acc_scale[part_index] = acc_scale[part_index] + grad_first
                    acc_shift[part_index] = acc_shift[part_index] + grad_second
        grad_group = [grad_rows]
        frames_list.append(jnp.stack(out_group))
        grads_list.append(jnp.stack(grad_group))
    total_qkv, total_out, total_up, total_down = (
        lax.psum(jnp.stack(acc_qkv).astype(jnp.bfloat16), "dp").astype(jnp.float32),
        lax.psum(jnp.stack(acc_out).astype(jnp.bfloat16), "dp").astype(jnp.float32),
        lax.psum(jnp.stack(acc_up).astype(jnp.bfloat16), "dp").astype(jnp.float32),
        lax.psum(jnp.stack(acc_down).astype(jnp.bfloat16), "dp").astype(jnp.float32),
    )
    norm_totals = lax.psum(
        (jnp.stack(acc_gain), jnp.stack(acc_bias), jnp.stack(acc_scale), jnp.stack(acc_shift)),
        ("dp", "tensor"),
    )
    return (
        jnp.stack(frames_list),
        jnp.stack(grads_list),
        total_qkv.reshape(2, model_width, 3, -1),
        total_out,
        total_up,
        total_down,
        norm_totals[0],
        norm_totals[1],
        norm_totals[2],
        norm_totals[3],
    )


def solution(mesh):
    return jax.shard_map(
        per_device,
        mesh=mesh,
        in_specs=(
            P(None, "dp", "tensor", None),
            P(None, "dp"),
            P(None, "dp"),
            P(None, "dp"),
            P(),
            P(),
            P(),
            P(),
            P(None, None, None, "tensor"),
            P(None, "tensor", None),
            P(None, None, "tensor"),
            P(None, "tensor", None),
            P(None, "dp", "tensor", None),
        ),
        out_specs=(
            P(None, "dp", "tensor", None),
            P(None, "dp", "tensor", None),
            P(None, None, None, "tensor"),
            P(None, "tensor", None),
            P(None, None, "tensor"),
            P(None, "tensor", None),
            P(),
            P(),
            P(),
            P(),
        ),
        check_vma=False,
    )
```

profile of v0, /device:TPU:0, one launch (start us, length us, event | category | flops | bytes accessed | tf_op | source)
XLA Modules:
  0.0 2267.6 jit_solution(17285633225396595511)
XLA Ops:
  28.0 22.1 all-gather.19.cloned.1.call-done
  63.6 38.0 %while.108 = (s32[]{:T(128)}, bf16[2,512,8,64]{1,3,2,0:T(8,128)(2,1)S(1)}, f32[2,8,512,1]{2,1,3,0:T(8,128)S(1)}, s32[]{:T(128)}, s32[]{:T(128)}, /*index=5*/s32[...) while((s32[]{:T(128)}, ...), condition=%wide.region_5.6_spmd, body=%wide.region_2.5_spmd.sunk | while | flops 1121712640 | bytes 55713984 | solution.py:103
  106.9 31.7 %reduce-scatter.17.cloned.1.call-done = bf16[512,1024]{1,0:T(8,128)(2,1)} async-done(((bf16[1024,1024]{1,0:T(8,128)(2,1)}), bf16[512,1024]{1,0:T(8,128)(2,1)}) %reduce-scatter.17.cloned.1.call-update) | async-done | bytes 1048592 | tf_op jit(solution)/shard_map/reduce_scatter | solution.py:43
  143.3 31.9 %all-gather.27.cloned.1.call-done = bf16[1024,1024]{1,0:T(8,128)(2,1)} async-done(((bf16[512,1024]{1,0:T(8,128)(2,1)}), bf16[1024,1024]{1,0:T(8,128)(2,1)}) %all-gather.27.cloned.1.call-update) | async-done | bytes 2097168 | tf_op jit(solution)/shard_map/all_gather | solution.py:35
  188.8 38.0 %while.110 = (s32[]{:T(128)}, bf16[2,512,8,64]{1,3,2,0:T(8,128)(2,1)S(1)}, f32[2,8,512,1]{2,1,3,0:T(8,128)S(1)}, s32[]{:T(128)}, s32[]{:T(128)}, /*index=5*/s32[...) while((s32[]{:T(128)}, ...), condition=%wide.region_25.26_spmd, body=%wide.region_22.25_spmd.sunk | while | flops 1121712640 | bytes 55713984 | solution.py:103
  232.1 31.7 %reduce-scatter.25.cloned.1.call-done = bf16[512,1024]{1,0:T(8,128)(2,1)} async-done(((bf16[1024,1024]{1,0:T(8,128)(2,1)}), bf16[512,1024]{1,0:T(8,128)(2,1)}) %reduce-scatter.25.cloned.1.call-update) | async-done | bytes 1048592 | tf_op jit(solution)/shard_map/reduce_scatter | solution.py:43
  269.9 32.6 %all-gather.29.cloned.1.call-done = bf16[1024,1024]{1,0:T(8,128)(2,1)} async-done(((bf16[512,1024]{1,0:T(8,128)(2,1)}), bf16[1024,1024]{1,0:T(8,128)(2,1)}) %all-gather.29.cloned.1.call-update) | async-done | bytes 2097168 | tf_op jit(solution)/shard_map/all_gather | solution.py:35
  322.4 15.3 all-gather.21.cloned.1.call-done
  360.2 12.1 reduce-scatter.27.cloned.1.call-done
  372.3 34.8 %reduce-scatter.19.cloned.1.call-done = bf16[512,1024]{1,0:T(8,128)(2,1)} async-done(((bf16[1024,1024]{1,0:T(8,128)(2,1)}), bf16[512,1024]{1,0:T(8,128)(2,1)}) %reduce-scatter.19.cloned.1.call-update) | async-done | bytes 1048592 | tf_op jit(solution)/shard_map/reduce_scatter | solution.py:43
  422.0 25.1 %all-gather.31.cloned.1.call-done = bf16[1024,1024]{1,0:T(8,128)(2,1)} async-done(((bf16[512,1024]{1,0:T(8,128)(2,1)}), bf16[1024,1024]{1,0:T(8,128)(2,1)}) %all-gather.31.cloned.1.call-update) | async-done | bytes 2097168 | tf_op jit(solution)/shard_map/all_gather | solution.py:35
  457.0 25.2 %all-gather.23.cloned.1.call-done = bf16[1024,1024]{1,0:T(8,128)(2,1)} async-done(((bf16[512,1024]{1,0:T(8,128)(2,1)}), bf16[1024,1024]{1,0:T(8,128)(2,1)}) %all-gather.23.cloned.1.call-update) | async-done | bytes 2097168 | tf_op jit(solution)/shard_map/all_gather | solution.py:35
  495.9 31.0 %while.109 = (s32[]{:T(128)}, bf16[2,512,8,64]{1,3,2,0:T(8,128)(2,1)}, f32[2,8,512,1]{2,1,3,0:T(8,128)S(1)}, s32[]{:T(128)}, s32[2]{0:T(128)S(1)}, /*index=5*/bf...) while((s32[]{:T(128)}, ...), condition=%wide.region_15.16_spmd, body=%wide.region_12.15_spmd.sunk | while | flops 1120138240 | bytes 66195716 | solution.py:103
  535.1 28.7 %while.111 = (s32[]{:T(128)}, bf16[2,512,8,64]{1,3,2,0:T(8,128)(2,1)}, f32[2,8,512,1]{2,1,3,0:T(8,128)S(1)}, s32[]{:T(128)}, s32[2]{0:T(128)S(1)}, /*index=5*/bf...) while((s32[]{:T(128)}, ...), condition=%wide.region_35.36_spmd, body=%wide.region_32.35_spmd.sunk | while | flops 1120138240 | bytes 62001388 | solution.py:103
  582.2 20.7 reduce-scatter.29.cloned.1.call-done
  607.2 30.9 %all-gather.25.cloned.1.call-done = bf16[1024,1024]{1,0:T(8,128)(2,1)} async-done(((bf16[512,1024]{1,0:T(8,128)(2,1)}), bf16[1024,1024]{1,0:T(8,128)(2,1)}) %all-gather.25.cloned.1.call-update) | async-done | bytes 2097168 | tf_op jit(solution)/shard_map/all_gather | solution.py:35
  638.2 10.9 fusion.158
  649.1 24.2 %all-gather.47.cloned.1.call-done = bf16[1,1,1024,1024]{3,2,1,0:T(8,128)(2,1)} async-done(((bf16[1,1,512,1024]{3,2,1,0:T(8,128)(2,1)}), bf16[1,1,1024,1024]{3,2,1,0:T(8,128)(2,1)}) %all-gather.47.cloned.1.call-update) | async-done | bytes 2097168 | tf_op jit(solution)/shard_map/all_gather | solution.py:49
  673.3 12.5 fusion.125
  696.2 11.0 fusion.275
  708.4 10.8 fusion.156
  719.2 23.7 %reduce-scatter.33.cloned.1.call-done = bf16[512,1024]{1,0:T(8,128)(2,1)} async-done(((bf16[1024,1024]{1,0:T(8,128)(2,1)}), bf16[512,1024]{1,0:T(8,128)(2,1)}) %reduce-scatter.33.cloned.1.call-update) | async-done | bytes 1048592 | tf_op jit(solution)/shard_map/reduce_scatter | solution.py:53
  745.6 31.3 %reduce-scatter.23.cloned.1.call-done = bf16[512,1024]{1,0:T(8,128)(2,1)} async-done(((bf16[1024,1024]{1,0:T(8,128)(2,1)}), bf16[512,1024]{1,0:T(8,128)(2,1)}) %reduce-scatter.23.cloned.1.call-update) | async-done | bytes 1048592 | tf_op jit(solution)/shard_map/reduce_scatter | solution.py:43
  783.4 28.2 %all-gather.49.cloned.1.call-done = bf16[1,1,1024,1024]{3,2,1,0:T(8,128)(2,1)} async-done(((bf16[1,1,512,1024]{3,2,1,0:T(8,128)(2,1)}), bf16[1,1,1024,1024]{3,2,1,0:T(8,128)(2,1)}) %all-gather.49.cloned.1.call-update) | async-done | bytes 2097168 | tf_op jit(solution)/shard_map/all_gather | solution.py:49
  811.5 12.5 fusion.139
  834.3 11.1 fusion.278
  851.8 86.9 %while.112 = (s32[]{:T(128)}, f32[1024,8,64]{0,2,1:T(8,128)}, f32[1024,8,64]{0,2,1:T(8,128)}, bf16[2,512,8,64]{1,3,2,0:T(8,128)(2,1)}, s32[2]{0:T(128)S(1)}, /*i...) while((s32[]{:T(128)}, f32[1024,8,64]{0,2,1:T(8,128)}, ...), condition=%wide.region_45.46_spmd.clone, body=%wide.region_43.45_spmd.clone.sunk | while | flops 2724983808 | bytes 207702432 | solution.py:145
  860.0 10.8 multiply_reduce_fusion.14
  870.8 9.5 multiply_convert_fusion.20
  902.9 10.8 multiply_reduce_fusion.14
  913.7 9.5 multiply_convert_fusion.20
  923.2 9.5 bitcast_add_fusion.17
  959.3 23.0 %reduce-scatter.35.cloned.1.call-done = bf16[512,1024]{1,0:T(8,128)(2,1)} async-done(((bf16[1024,1024]{1,0:T(8,128)(2,1)}), bf16[512,1024]{1,0:T(8,128)(2,1)}) %reduce-scatter.35.cloned.1.call-update) | async-done | bytes 1048592 | tf_op jit(solution)/shard_map/reduce_scatter | solution.py:53
  991.6 33.2 %all-gather.41.cloned.1.call-done = bf16[1024,1024]{1,0:T(8,128)(2,1)} async-done(((bf16[512,1024]{1,0:T(8,128)(2,1)}), bf16[1024,1024]{1,0:T(8,128)(2,1)}) %all-gather.41.cloned.1.call-update) | async-done | bytes 2097168 | tf_op jit(solution)/shard_map/all_gather | solution.py:49
  1030.1 86.5 %while.114 = (s32[]{:T(128)}, f32[1024,8,64]{0,2,1:T(8,128)}, f32[1024,8,64]{0,2,1:T(8,128)}, bf16[2,512,8,64]{1,3,2,0:T(8,128)(2,1)}, s32[2]{0:T(128)S(1)}, /*i...) while((s32[]{:T(128)}, f32[1024,8,64]{0,2,1:T(8,128)}, ...), condition=%wide.region_63.64_spmd.clone, body=%wide.region_61.63_spmd.clone.sunk | while | flops 2724983808 | bytes 207702432 | solution.py:145
  1038.1 10.8 multiply_reduce_fusion.16
  1080.9 10.8 multiply_reduce_fusion.16
  1137.2 11.8 fusion.143
  1149.1 10.9 fusion.382
  1167.0 27.6 %all-gather.37.cloned.1.call-done = bf16[1024,1024]{1,0:T(8,128)(2,1)} async-done(((bf16[512,1024]{1,0:T(8,128)(2,1)}), bf16[1024,1024]{1,0:T(8,128)(2,1)}) %all-gather.37.cloned.1.call-update) | async-done | bytes 2097168 | tf_op jit(solution)/shard_map/all_gather | solution.py:49
  1194.6 12.5 fusion.118
  1217.4 12.0 fusion.141
  1236.6 13.2 fusion.132
  1280.7 12.9 fusion.355
  1308.6 14.1 fusion.142
  1346.4 114.4 %while.115 = (s32[]{:T(128)}, f32[1024,8,64]{0,2,1:T(8,128)}, f32[1024,8,64]{0,2,1:T(8,128)}, bf16[2,512,8,64]{1,3,2,0:T(8,128)(2,1)}, s32[2]{0:T(128)S(1)}, /*i...) while((s32[]{:T(128)}, f32[1024,8,64]{0,2,1:T(8,128)}, ...), condition=%wide.region_72.73_spmd.clone, body=%wide.region_70.72_spmd.clone.sunk | while | flops 2726558208 | bytes 225534288 | solution.py:145
  1350.9 10.2 fusion.588
  1361.2 13.5 multiply_reduce_fusion.17
  1374.7 11.5 multiply_convert_fusion.23
  1407.6 10.0 fusion.588
  1417.6 13.5 multiply_reduce_fusion.17
  1431.1 11.5 multiply_convert_fusion.23
  1476.4 114.0 %while.113 = (s32[]{:T(128)}, f32[1024,8,64]{0,2,1:T(8,128)}, f32[1024,8,64]{0,2,1:T(8,128)}, bf16[2,512,8,64]{1,3,2,0:T(8,128)(2,1)}, s32[2]{0:T(128)S(1)}, /*i...) while((s32[]{:T(128)}, f32[1024,8,64]{0,2,1:T(8,128)}, ...), condition=%wide.region_54.55_spmd.clone, body=%wide.region_52.54_spmd.clone.sunk | while | flops 2726558208 | bytes 225534288 | solution.py:145
  1480.8 10.1 fusion.565
  1490.9 13.6 multiply_reduce_fusion.15
  1504.5 11.5 multiply_convert_fusion.21
  1537.5 10.0 fusion.565
  1547.5 13.5 multiply_reduce_fusion.15
  1561.0 11.5 multiply_convert_fusion.21
  1600.6 12.0 fusion.140
  1673.6 98.0 %all-reduce.5.cloned.1.call-done = (f32[2,1024]{1,0:T(2,128)}, f32[2,1024]{1,0:T(2,128)}, f32[2,7,1024]{2,1,0:T(8,128)}, f32[2,7,1024]{2,1,0:T(8,128)}) async-done(((f32[2,1024]{1,0:T(2,128)}, f32[2,1024]{1,0:T(2,128)}, f32[2,7,1024]{2,1,0:T(8,128)}, f32[2,7,1024]{2,1,0:T(8,128)}), (f32[2,1024]{1,0:T(2,128)}, f32[2,1024]{1,0:T(2,128)}, f32[2,7,1024]{2,1,0:T(8,128)}, ...) | async-done | bytes 131088 | tf_op jit(solution)/shard_map/psum | solution.py:313
  1774.6 447.7 %all-reduce.7.cloned.1.call-done = (bf16[2,1024,3,512]{1,3,2,0:T(8,128)(2,1)}, bf16[2,512,1024]{2,1,0:T(8,128)(2,1)}, bf16[2,1024,2048]{2,1,0:T(8,128)(2,1)}, bf16[2,2048,1024]{2,1,0:T(8,128)(2,1)}) async-done(((bf16[2,1024,3,512]{1,3,2,0:T(8,128)(2,1)}, bf16[2,512,1024]{2,1,0:T(8,128)(2,1)}, bf16[2,1024,2048]{2,1,0:T(8,128)(2,1)}, bf16[2,2048,1024]{2,1,0:T(8,128)(2,1)}), ...) | async-done | bytes 25165840 | tf_op jit(solution)/shard_map/psum | solution.py:308
  2235.7 11.7 convert_element_type.355
  2247.4 11.7 convert_element_type.356
  (902 shorter events, 759.0 us)
Async XLA Ops:
  7.2 42.9 %all-gather.19.cloned.1.call-start = ((), (), s32[]{:S(2)}) async-start(), calls=%async_computation.16 | async-start | bytes 3145728 | tf_op jit(solution)/shard_map/all_gather | solution.py:35
  12.1 128.4 %copy-start.116 = (f32[1,1024]{1,0:T(1,128)}, f32[1,1024]{1,0:T(1,128)S(1)}, u32[]{:S(2)}) copy-start(f32[1,1024]{1,0:T(1,128)S(1)} %get-tuple-element.998) | copy-start | bytes 12292
  14.1 124.5 %reduce-scatter.17.cloned.1.call-start = ((), (), s32[]{:S(2)}) async-start(), calls=%async_computation.17 | async-start | bytes 3145728 | tf_op jit(solution)/shard_map/reduce_scatter | solution.py:43
  106.7 68.6 %all-gather.27.cloned.1.call-start = ((), (), s32[]{:S(2)}) async-start(), calls=%async_computation.24 | async-start | bytes 3145728 | tf_op jit(solution)/shard_map/all_gather | solution.py:35
  106.9 35.1 %copy-start.124 = (f32[512]{0:T(512)}, f32[512]{0:T(512)S(1)}, u32[]{:S(2)}) copy-start(f32[512]{0:T(512)S(1)} %broadcast_multiply_fusion.3) | copy-start | bytes 6148
  140.5 34.8 %copy-start.164 = (f32[512]{0:T(512)}, f32[512]{0:T(512)S(1)}, u32[]{:S(2)}) copy-start(f32[512]{0:T(512)S(1)} %get-tuple-element.733) | copy-start | bytes 6148
  140.5 34.7 %copy-start.144 = (f32[512]{0:T(512)}, f32[512]{0:T(512)S(1)}, u32[]{:S(2)}) copy-start(f32[512]{0:T(512)S(1)} %fusion.331) | copy-start | bytes 6148
  142.0 121.8 %reduce-scatter.25.cloned.1.call-start = ((), (), s32[]{:S(2)}) async-start(), calls=%async_computation.25 | async-start | bytes 3145728 | tf_op jit(solution)/shard_map/reduce_scatter | solution.py:43
  229.2 34.6 %copy-start.40 = (bf16[512,1024]{1,0:T(8,128)(2,1)S(1)}, bf16[512,1024]{1,0:T(8,128)(2,1)}, u32[]{:S(2)}) copy-start(bf16[512,1024]{1,0:T(8,128)(2,1)} %reduce-scatter.17.cloned.1.call-done) | copy-start | bytes 3145732
  231.8 70.7 %all-gather.29.cloned.1.call-start = ((), (), s32[]{:S(2)}) async-start(), calls=%async_computation.26 | async-start | bytes 3145728 | tf_op jit(solution)/shard_map/all_gather | solution.py:35
  232.1 34.9 %copy-start.136 = (f32[512]{0:T(512)}, f32[512]{0:T(512)S(1)}, u32[]{:S(2)}) copy-start(f32[512]{0:T(512)S(1)} %broadcast_multiply_fusion.6) | copy-start | bytes 6148
  232.1 34.9 %copy-start.132 = (f32[1,1024]{1,0:T(1,128)S(1)}, f32[1,1024]{1,0:T(1,128)}, u32[]{:S(2)}) copy-start(f32[1,1024]{1,0:T(1,128)} %get-tuple-element.997) | copy-start | bytes 12292
  232.1 34.9 %copy-start.188 = (f32[1,1024]{1,0:T(1,128)S(1)}, f32[1,1024]{1,0:T(1,128)}, u32[]{:S(2)}) copy-start(f32[1,1024]{1,0:T(1,128)} %get-tuple-element.999) | copy-start | bytes 12292
  269.3 68.4 %all-gather.21.cloned.1.call-start = ((), (), s32[]{:S(2)}) async-start(), calls=%async_computation.18 | async-start | bytes 3145728 | tf_op jit(solution)/shard_map/all_gather | solution.py:35
  269.8 102.5 %reduce-scatter.27.cloned.1.call-start = ((), (), s32[]{:S(2)}) async-start(), calls=%async_computation.27 | async-start | bytes 3145728 | tf_op jit(solution)/shard_map/reduce_scatter | solution.py:43
  322.0 85.2 %reduce-scatter.19.cloned.1.call-start = ((), (), s32[]{:S(2)}) async-start(), calls=%async_computation.19 | async-start | bytes 3145728 | tf_op jit(solution)/shard_map/reduce_scatter | solution.py:43
  356.8 90.3 %all-gather.31.cloned.1.call-start = ((), (), s32[]{:S(2)}) async-start(), calls=%async_computation.28 | async-start | bytes 3145728 | tf_op jit(solution)/shard_map/all_gather | solution.py:35
  358.8 52.7 %copy-start.118 = (f32[1,1024]{1,0:T(1,128)}, f32[1,1024]{1,0:T(1,128)S(1)}, u32[]{:S(2)}) copy-start(f32[1,1024]{1,0:T(1,128)S(1)} %fusion.317) | copy-start | bytes 12292
  413.8 68.4 %all-gather.23.cloned.1.call-start = ((), (), s32[]{:S(2)}) async-start(), calls=%async_computation.20 | async-start | bytes 3145728 | tf_op jit(solution)/shard_map/all_gather | solution.py:35
  418.4 154.2 %reduce-scatter.21.cloned.1.call-start = ((), (), s32[]{:S(2)}) async-start(), calls=%async_computation.21 | async-start | bytes 3145728 | tf_op jit(solution)/shard_map/reduce_scatter | solution.py:43
  422.0 25.1 %copy-start.79 = (bf16[1,1024,3,512]{1,3,2,0:T(8,128)(2,1)}, bf16[1,1024,3,512]{1,3,2,0:T(8,128)(2,1)S(1)}, u32[]{:S(2)}) copy-start(bf16[1,1024,3,512]{1,3,2,0:T(8,128)(2,1)S(1)} %copy.83) | copy-start | bytes 9437188
  533.6 69.3 %reduce-scatter.29.cloned.1.call-start = ((), (), s32[]{:S(2)}) async-start(), calls=%async_computation.29 | async-start | bytes 3145728 | tf_op jit(solution)/shard_map/reduce_scatter | solution.py:43
  570.8 67.4 %all-gather.25.cloned.1.call-start = ((), (), s32[]{:S(2)}) async-start(), calls=%async_computation.22 | async-start | bytes 3145728 | tf_op jit(solution)/shard_map/all_gather | solution.py:35
  576.8 26.1 %copy-start.27 = (f32[512,1024]{1,0:T(8,128)S(1)}, f32[512,1024]{1,0:T(8,128)}, u32[]{:S(2)}) copy-start(f32[512,1024]{1,0:T(8,128)} %copy-done.26) | copy-start | bytes 6291460
  576.8 96.5 %all-gather.47.cloned.1.call-start = ((), (), s32[]{:S(2)}) async-start(), calls=%async_computation.46 | async-start | bytes 3145728 | tf_op jit(solution)/shard_map/all_gather | solution.py:49
  580.3 128.1 %all-gather.33.cloned.1.call-start = ((), (), s32[]{:S(2)}) async-start(), calls=%async_computation.30 | async-start | bytes 3145728 | tf_op jit(solution)/shard_map/all_gather | solution.py:35
  581.5 23.3 %copy-start.130 = (f32[1,1024]{1,0:T(1,128)}, f32[1,1024]{1,0:T(1,128)S(1)}, u32[]{:S(2)}) copy-start(f32[1,1024]{1,0:T(1,128)S(1)} %fusion.313) | copy-start | bytes 12292
  604.8 44.3 %copy-start.172 = (f32[512]{0:T(512)}, f32[512]{0:T(512)S(1)}, u32[]{:S(2)}) copy-start(f32[512]{0:T(512)S(1)} %multiply_reduce_fusion.4) | copy-start | bytes 6148
  604.8 44.3 %copy-start.150 = (f32[512]{0:T(512)}, f32[512]{0:T(512)S(1)}, u32[]{:S(2)}) copy-start(f32[512]{0:T(512)S(1)} %fusion.334) | copy-start | bytes 6148
  607.2 135.7 %reduce-scatter.33.cloned.1.call-start = ((), (), s32[]{:S(2)}) async-start(), calls=%async_computation.32 | async-start | bytes 3145728 | tf_op jit(solution)/shard_map/reduce_scatter | solution.py:53
  696.0 81.0 %reduce-scatter.23.cloned.1.call-start = ((), (), s32[]{:S(2)}) async-start(), calls=%async_computation.23 | async-start | bytes 3145728 | tf_op jit(solution)/shard_map/reduce_scatter | solution.py:43
  707.2 104.4 %all-gather.49.cloned.1.call-start = ((), (), s32[]{:S(2)}) async-start(), calls=%async_computation.47 | async-start | bytes 3145728 | tf_op jit(solution)/shard_map/all_gather | solution.py:49
  707.8 35.2 %copy-start.39 = (f32[512,1024]{1,0:T(8,128)S(1)}, f32[512,1024]{1,0:T(8,128)}, u32[]{:S(2)}) copy-start(f32[512,1024]{1,0:T(8,128)} %copy-done.38) | copy-start | bytes 6291460
  707.8 139.0 %all-gather.35.cloned.1.call-start = ((), (), s32[]{:S(2)}) async-start(), calls=%async_computation.33 | async-start | bytes 3145728 | tf_op jit(solution)/shard_map/all_gather | solution.py:49
  742.9 34.1 %copy-start.67 = (bf16[512,1024]{1,0:T(8,128)(2,1)S(1)}, bf16[512,1024]{1,0:T(8,128)(2,1)}, u32[]{:S(2)}) copy-start(bf16[512,1024]{1,0:T(8,128)(2,1)} %reduce-scatter.33.cloned.1.call-done) | copy-start | bytes 3145732
  783.1 167.0 %reduce-scatter.41.cloned.1.call-start = ((), (), s32[]{:S(2)}) async-start(), calls=%async_computation.39 | async-start | bytes 3145728 | tf_op jit(solution)/shard_map/reduce_scatter | solution.py:53
  834.2 120.2 %reduce-scatter.31.cloned.1.call-start = ((), (), s32[]{:S(2)}) async-start(), calls=%async_computation.31 | async-start | bytes 3145728 | tf_op jit(solution)/shard_map/reduce_scatter | solution.py:43
  845.4 136.8 %reduce-scatter.35.cloned.1.call-start = ((), (), s32[]{:S(2)}) async-start(), calls=%async_computation.34 | async-start | bytes 3145728 | tf_op jit(solution)/shard_map/reduce_scatter | solution.py:53
  950.1 74.8 %all-gather.41.cloned.1.call-start = ((), (), s32[]{:S(2)}) async-start(), calls=%async_computation.40 | async-start | bytes 3145728 | tf_op jit(solution)/shard_map/all_gather | solution.py:49
  954.3 27.9 %copy-start.25 = (f32[512,1024]{1,0:T(8,128)S(1)}, f32[512,1024]{1,0:T(8,128)}, u32[]{:S(2)}) copy-start(f32[512,1024]{1,0:T(8,128)} %get-tuple-element.937) | copy-start | bytes 6291460
  954.4 27.9 %copy-start.121 = (f32[1,1024]{1,0:T(1,128)S(1)}, f32[1,1024]{1,0:T(1,128)}, u32[]{:S(2)}) copy-start(f32[1,1024]{1,0:T(1,128)} %copy-done.120) | copy-start | bytes 12292
  954.4 27.9 %copy-start.129 = (f32[512]{0:T(512)S(1)}, f32[512]{0:T(512)}, u32[]{:S(2)}) copy-start(f32[512]{0:T(512)} %copy-done.128) | copy-start | bytes 6148
  959.2 25.6 %copy-start.171 = (f32[512]{0:T(512)S(1)}, f32[512]{0:T(512)}, u32[]{:S(2)}) copy-start(f32[512]{0:T(512)} %copy-done.170) | copy-start | bytes 6148
  959.2 25.7 %copy-start.155 = (f32[512]{0:T(512)S(1)}, f32[512]{0:T(512)}, u32[]{:S(2)}) copy-start(f32[512]{0:T(512)} %copy-done.154) | copy-start | bytes 6148
  959.3 28.6 %copy-start.176 = (f32[512]{0:T(512)}, f32[512]{0:T(512)S(1)}, u32[]{:S(2)}) copy-start(f32[512]{0:T(512)S(1)} %negate_multiply_fusion.3) | copy-start | bytes 6148
  959.3 28.6 %copy-start.175 = (f32[512]{0:T(512)S(1)}, f32[512]{0:T(512)}, u32[]{:S(2)}) copy-start(f32[512]{0:T(512)} %copy-done.174) | copy-start | bytes 6148
  991.5 168.5 %reduce-scatter.43.cloned.1.call-start = ((), (), s32[]{:S(2)}) async-start(), calls=%async_computation.41 | async-start | bytes 3145728 | tf_op jit(solution)/shard_map/reduce_scatter | solution.py:53
  991.6 38.5 %copy-start.8 = (bf16[1024,8,64]{0,2,1:T(8,128)(2,1)S(1)}, bf16[1024,8,64]{0,2,1:T(8,128)(2,1)}, u32[]{:S(2)}) copy-start(bf16[1024,8,64]{0,2,1:T(8,128)(2,1)} %copy-done.7) | copy-start | bytes 3145732
  1127.9 66.7 %all-gather.37.cloned.1.call-start = ((), (), s32[]{:S(2)}) async-start(), calls=%async_computation.35 | async-start | bytes 3145728 | tf_op jit(solution)/shard_map/all_gather | solution.py:49
  1149.1 87.5 %all-gather.43.cloned.1.call-start = ((), (), s32[]{:S(2)}) async-start(), calls=%async_computation.42 | async-start | bytes 3145728 | tf_op jit(solution)/shard_map/all_gather | solution.py:49
  1166.8 128.1 %reduce-scatter.37.cloned.1.call-start = ((), (), s32[]{:S(2)}) async-start(), calls=%async_computation.36 | async-start | bytes 3145728 | tf_op jit(solution)/shard_map/reduce_scatter | solution.py:53
  1217.3 80.6 %reduce-scatter.45.cloned.1.call-start = ((), (), s32[]{:S(2)}) async-start(), calls=%async_computation.43 | async-start | bytes 3145728 | tf_op jit(solution)/shard_map/reduce_scatter | solution.py:53
  1260.1 81.0 %all-gather.45.cloned.1.call-start = ((), (), s32[]{:S(2)}) async-start(), calls=%async_computation.44 | async-start | bytes 3145728 | tf_op jit(solution)/shard_map/all_gather | solution.py:49
  1280.6 17.3 copy-start.5
  1280.6 17.3 copy-start.41
  1280.6 17.3 copy-start.133
  1280.6 17.3 copy-start.137
  1280.6 17.3 copy-start.139
  1280.6 17.3 copy-start.147
  1307.9 163.6 %all-gather.39.cloned.1.call-start = ((), (), s32[]{:S(2)}) async-start(), calls=%async_computation.37 | async-start | bytes 3145728 | tf_op jit(solution)/shard_map/all_gather | solution.py:49
  1332.2 310.5 %reduce-scatter.47.cloned.1.call-start = ((), (), s32[]{:S(2)}) async-start(), calls=%async_computation.45 | async-start | bytes 3145728 | tf_op jit(solution)/shard_map/reduce_scatter | solution.py:53
  1471.4 171.4 %reduce-scatter.39.cloned.1.call-start = ((), (), s32[]{:S(2)}) async-start(), calls=%async_computation.38 | async-start | bytes 3145728 | tf_op jit(solution)/shard_map/reduce_scatter | solution.py:53
  1600.5 171.1 %all-reduce.5.cloned.1.call-start = ((), (), s32[]{:S(2)}) async-start(), calls=%async_computation.48 | async-start | bytes 294912 | tf_op jit(solution)/shard_map/psum | solution.py:313
  1649.7 572.6 %all-reduce.7.cloned.1.call-start = ((), (), s32[]{:S(2)}) async-start(), calls=%async_computation.49 | async-start | bytes 50331648 | tf_op jit(solution)/shard_map/psum | solution.py:308
  (219 other events, 1108.4 us)
Sparse Core Ops, SparseCore 0:
  14.3 35.8 all-gather.18
  106.8 31.8 reduce-scatter.16
  142.1 33.1 all-gather.26
  231.9 31.8 reduce-scatter.24
  269.4 33.1 all-gather.28
  304.5 33.1 all-gather.20
  340.5 31.8 reduce-scatter.26
  375.2 31.8 reduce-scatter.18
  413.9 33.1 all-gather.30
  449.0 33.1 all-gather.22
  533.7 31.8 reduce-scatter.20
  570.9 31.9 reduce-scatter.28
  605.0 33.1 all-gather.24
  640.1 33.1 all-gather.46
  675.3 33.1 all-gather.32
  711.1 31.8 reduce-scatter.32
  745.1 31.8 reduce-scatter.22
  778.4 33.1 all-gather.48
  813.7 33.1 all-gather.34
  848.9 31.8 reduce-scatter.40
  883.1 31.8 reduce-scatter.30
  950.2 32.0 reduce-scatter.34
  991.7 33.1 all-gather.40
  1128.0 31.8 reduce-scatter.42
  1161.5 33.1 all-gather.36
  1196.6 33.1 all-gather.42
  1231.8 31.8 reduce-scatter.36
  1266.0 31.8 reduce-scatter.44
  1308.0 33.1 all-gather.44
  1342.6 33.1 all-gather.38
  1471.5 31.8 reduce-scatter.46
  1600.6 31.7 reduce-scatter.38
  1649.8 121.7 all-reduce.4
  1777.0 445.1 all-reduce.6
where the time goes:
time: 2280 us; the launch traced here: 2270 us
  waiting for transfers between devices  1070 us (47%)
  matrix products  689 us (30%)
  other arithmetic  272 us (12%)
  local copies, waits for them, and re-layouts  182 us (8%)
  loops' own time  33.7 us (1%)
    psum x1, waiting for transfers between devices, per_device(): lax.psum(jnp.stack(acc_qkv).astype(jnp.bfloat16), 'dp').astype(jnp.float32)  448 us
    all_gather x8, waiting for transfers between devices, gather_normed(): return lax.all_gather(normed_low, 'tensor', axis=0, tiled=True)  184 us
    reduce_scatter x8, waiting for transfers between devices, sum_branch(): lax.psum_scatter(branch_part.astype(jnp.bfloat16), 'tensor', scatter_dime...  162 us
    dot_general x16, matrix products, block_scores(): jnp.einsum('qhd,khd->hqk', query_block, key_rows, preferred_element_type=...  130 us
    all_gather x8, waiting for transfers between devices, gather_grad(): return lax.all_gather(grad_low, 'tensor', axis=0, tiled=True)  123 us
    psum x1, waiting for transfers between devices, per_device(): lax.psum((jnp.stack(acc_gain), jnp.stack(acc_bias), jnp.stack(acc_scale),...  98 us
    convert_element_type x8, other arithmetic, one_block(): grad_scores = (shares * (grad_shares - inner_sum)).astype(jnp.bfloat16)  83.9 us
    unnamed x413, local copies, waits for them, and re-layouts  63.4 us
  transfers between devices with their start and end apart: 34, of which 25 were waited for; matrix products, arithmetic and copies ran while one was open for 33% of the time, Pallas kernels for 0%

commit v1 on v0

--- a/solution.py
+++ b/solution.py
@@ -304,8 +304,12 @@
         grad_group = [grad_rows]
         frames_list.append(jnp.stack(out_group))
         grads_list.append(jnp.stack(grad_group))
+
+    def masks_convert(array_in, shard_axis):
+        return jnp.sum(lax.all_gather(array_in, shard_axis), 0)
+
     total_qkv, total_out, total_up, total_down = (
-        lax.psum(jnp.stack(acc_qkv).astype(jnp.bfloat16), "dp").astype(jnp.float32),
+        masks_convert(jnp.stack(acc_qkv).astype(jnp.bfloat16), "dp").astype(jnp.float32),
         lax.psum(jnp.stack(acc_out).astype(jnp.bfloat16), "dp").astype(jnp.float32),
         lax.psum(jnp.stack(acc_up).astype(jnp.bfloat16), "dp").astype(jnp.float32),
         lax.psum(jnp.stack(acc_down).astype(jnp.bfloat16), "dp").astype(jnp.float32),

time: 2280 us -> 2670 us (1.17)
  waiting for transfers between devices: 1070 us -> 1430 us
  other arithmetic: 272 us -> 308 us
    all_gather x0 -> x1, waiting for transfers between devices: none -> 457 us  [masks_convert(): return jnp.sum(lax.all_gather(array_in, shard_axis), 0)]
    psum x1, waiting for transfers between devices: 448 us -> 335 us  [per_device(): lax.psum(jnp.stack(acc_out).astype(jnp.bfloat16), 'dp').astype(jnp.float32)]
    reduce_sum x0 -> x1, other arithmetic: none -> 35.2 us  [masks_convert(): return jnp.sum(lax.all_gather(array_in, shard_axis), 0)]
    unnamed x413 -> x421, local copies, waits for them, and re-layouts: 63.4 us -> 65.5 us
  transfers between devices with their start and end apart: 34 -> 35, of which waited for: 25 -> 28; matrix products, arithmetic and copies ran while one was open for 33% -> 29% of each run, Pallas kernels for 0% -> 0%
where the time goes in v1:
time: 2670 us; the launch traced here: 2660 us
  waiting for transfers between devices  1430 us (54%)
  matrix products  681 us (26%)
  other arithmetic  308 us (12%)
  local copies, waits for them, and re-layouts  185 us (7%)
  loops' own time  33.6 us (1%)
    all_gather x1, waiting for transfers between devices, masks_convert(): return jnp.sum(lax.all_gather(array_in, shard_axis), 0)  457 us
    psum x1, waiting for transfers between devices, per_device(): lax.psum(jnp.stack(acc_out).astype(jnp.bfloat16), 'dp').astype(jnp.float32)  335 us
    all_gather x8, waiting for transfers between devices, gather_normed(): return lax.all_gather(normed_low, 'tensor', axis=0, tiled=True)  184 us
    reduce_scatter x8, waiting for transfers between devices, sum_branch(): lax.psum_scatter(branch_part.astype(jnp.bfloat16), 'tensor', scatter_dime...  162 us
    all_gather x8, waiting for transfers between devices, gather_grad(): return lax.all_gather(grad_low, 'tensor', axis=0, tiled=True)  134 us
    dot_general x16, matrix products, block_scores(): jnp.einsum('qhd,khd->hqk', query_block, key_rows, preferred_element_type=...  130 us
    convert_element_type x8, other arithmetic, one_block(): grad_scores = (shares * (grad_shares - inner_sum)).astype(jnp.bfloat16)  83.8 us
    psum x1, waiting for transfers between devices, per_device(): lax.psum((jnp.stack(acc_gain), jnp.stack(acc_bias), jnp.stack(acc_scale),...  82.2 us
  transfers between devices with their start and end apart: 35, of which 28 were waited for; matrix products, arithmetic and copies ran while one was open for 29% of the time, Pallas kernels for 0%

profile of v1, /device:TPU:0, one launch (start us, length us, event | category | flops | bytes accessed | tf_op | source)
XLA Modules:
  0.0 2661.1 jit_solution(7391442716260046762)
XLA Ops:
  27.9 22.2 all-gather.20.cloned.1.call-done
  63.6 38.0 %while.108 = (s32[]{:T(128)}, bf16[2,512,8,64]{1,3,2,0:T(8,128)(2,1)S(1)}, f32[2,8,512,1]{2,1,3,0:T(8,128)S(1)}, s32[]{:T(128)}, s32[]{:T(128)}, /*index=5*/s32[...) while((s32[]{:T(128)}, ...), condition=%wide.region_5.6_spmd, body=%wide.region_2.5_spmd.sunk | while | flops 1121712640 | bytes 55713984 | solution.py:103
  107.2 31.4 %reduce-scatter.17.cloned.1.call-done = bf16[512,1024]{1,0:T(8,128)(2,1)} async-done(((bf16[1024,1024]{1,0:T(8,128)(2,1)}), bf16[512,1024]{1,0:T(8,128)(2,1)}) %reduce-scatter.17.cloned.1.call-update) | async-done | bytes 1048592 | tf_op jit(solution)/shard_map/reduce_scatter | solution.py:43
  143.3 31.9 %all-gather.28.cloned.1.call-done = bf16[1024,1024]{1,0:T(8,128)(2,1)} async-done(((bf16[512,1024]{1,0:T(8,128)(2,1)}), bf16[1024,1024]{1,0:T(8,128)(2,1)}) %all-gather.28.cloned.1.call-update) | async-done | bytes 2097168 | tf_op jit(solution)/shard_map/all_gather | solution.py:35
  188.7 37.9 %while.110 = (s32[]{:T(128)}, bf16[2,512,8,64]{1,3,2,0:T(8,128)(2,1)S(1)}, f32[2,8,512,1]{2,1,3,0:T(8,128)S(1)}, s32[]{:T(128)}, s32[]{:T(128)}, /*index=5*/s32[...) while((s32[]{:T(128)}, ...), condition=%wide.region_25.26_spmd, body=%wide.region_22.25_spmd.sunk | while | flops 1121712640 | bytes 55713984 | solution.py:103
  231.8 31.7 %reduce-scatter.25.cloned.1.call-done = bf16[512,1024]{1,0:T(8,128)(2,1)} async-done(((bf16[1024,1024]{1,0:T(8,128)(2,1)}), bf16[512,1024]{1,0:T(8,128)(2,1)}) %reduce-scatter.25.cloned.1.call-update) | async-done | bytes 1048592 | tf_op jit(solution)/shard_map/reduce_scatter | solution.py:43
  269.7 32.6 %all-gather.30.cloned.1.call-done = bf16[1024,1024]{1,0:T(8,128)(2,1)} async-done(((bf16[512,1024]{1,0:T(8,128)(2,1)}), bf16[1024,1024]{1,0:T(8,128)(2,1)}) %all-gather.30.cloned.1.call-update) | async-done | bytes 2097168 | tf_op jit(solution)/shard_map/all_gather | solution.py:35
  322.0 15.4 all-gather.22.cloned.1.call-done
  360.1 12.0 reduce-scatter.27.cloned.1.call-done
  372.1 34.8 %reduce-scatter.19.cloned.1.call-done = bf16[512,1024]{1,0:T(8,128)(2,1)} async-done(((bf16[1024,1024]{1,0:T(8,128)(2,1)}), bf16[512,1024]{1,0:T(8,128)(2,1)}) %reduce-scatter.19.cloned.1.call-update) | async-done | bytes 1048592 | tf_op jit(solution)/shard_map/reduce_scatter | solution.py:43
  422.0 24.8 all-gather.32.cloned.1.call-done
  456.7 25.2 all-gather.24.cloned.1.call-done
  495.6 31.0 %while.109 = (s32[]{:T(128)}, bf16[2,512,8,64]{1,3,2,0:T(8,128)(2,1)}, f32[2,8,512,1]{2,1,3,0:T(8,128)S(1)}, s32[]{:T(128)}, s32[2]{0:T(128)S(1)}, /*index=5*/bf...) while((s32[]{:T(128)}, ...), condition=%wide.region_15.16_spmd, body=%wide.region_12.15_spmd.sunk | while | flops 1120138240 | bytes 66195716 | solution.py:103
  534.7 28.7 %while.111 = (s32[]{:T(128)}, bf16[2,512,8,64]{1,3,2,0:T(8,128)(2,1)}, f32[2,8,512,1]{2,1,3,0:T(8,128)S(1)}, s32[]{:T(128)}, s32[2]{0:T(128)S(1)}, /*index=5*/bf...) while((s32[]{:T(128)}, ...), condition=%wide.region_35.36_spmd, body=%wide.region_32.35_spmd.sunk | while | flops 1120138240 | bytes 62001388 | solution.py:103
  581.6 20.7 reduce-scatter.29.cloned.1.call-done
  606.7 31.0 %all-gather.26.cloned.1.call-done = bf16[1024,1024]{1,0:T(8,128)(2,1)} async-done(((bf16[512,1024]{1,0:T(8,128)(2,1)}), bf16[1024,1024]{1,0:T(8,128)(2,1)}) %all-gather.26.cloned.1.call-update) | async-done | bytes 2097168 | tf_op jit(solution)/shard_map/all_gather | solution.py:35
  637.6 10.9 fusion.158
  648.5 24.2 all-gather.50.cloned.1.call-done
  672.8 12.5 fusion.125
  695.9 11.0 fusion.275
  707.9 11.0 fusion.156
  718.9 23.5 reduce-scatter.33.cloned.1.call-done
  745.1 31.3 %reduce-scatter.23.cloned.1.call-done = bf16[512,1024]{1,0:T(8,128)(2,1)} async-done(((bf16[1024,1024]{1,0:T(8,128)(2,1)}), bf16[512,1024]{1,0:T(8,128)(2,1)}) %reduce-scatter.23.cloned.1.call-update) | async-done | bytes 1048592 | tf_op jit(solution)/shard_map/reduce_scatter | solution.py:43
  782.9 28.1 %all-gather.52.cloned.1.call-done = bf16[1,1,1024,1024]{3,2,1,0:T(8,128)(2,1)} async-done(((bf16[1,1,512,1024]{3,2,1,0:T(8,128)(2,1)}), bf16[1,1,1024,1024]{3,2,1,0:T(8,128)(2,1)}) %all-gather.52.cloned.1.call-update) | async-done | bytes 2097168 | tf_op jit(solution)/shard_map/all_gather | solution.py:49
  811.0 12.5 fusion.139
  833.7 11.1 fusion.278
  851.2 86.7 %while.112 = (s32[]{:T(128)}, f32[1024,8,64]{0,2,1:T(8,128)}, f32[1024,8,64]{0,2,1:T(8,128)}, bf16[2,512,8,64]{1,3,2,0:T(8,128)(2,1)}, s32[2]{0:T(128)S(1)}, /*i...) while((s32[]{:T(128)}, f32[1024,8,64]{0,2,1:T(8,128)}, ...), condition=%wide.region_45.46_spmd.clone, body=%wide.region_43.45_spmd.clone.sunk | while | flops 2724983808 | bytes 207702432 | solution.py:145
  859.2 10.8 multiply_reduce_fusion.14
  902.1 10.8 multiply_reduce_fusion.14
  958.8 23.1 reduce-scatter.35.cloned.1.call-done
  991.2 33.2 %all-gather.42.cloned.1.call-done = bf16[1024,1024]{1,0:T(8,128)(2,1)} async-done(((bf16[512,1024]{1,0:T(8,128)(2,1)}), bf16[1024,1024]{1,0:T(8,128)(2,1)}) %all-gather.42.cloned.1.call-update) | async-done | bytes 2097168 | tf_op jit(solution)/shard_map/all_gather | solution.py:49
  1029.6 86.6 %while.114 = (s32[]{:T(128)}, f32[1024,8,64]{0,2,1:T(8,128)}, f32[1024,8,64]{0,2,1:T(8,128)}, bf16[2,512,8,64]{1,3,2,0:T(8,128)(2,1)}, s32[2]{0:T(128)S(1)}, /*i...) while((s32[]{:T(128)}, f32[1024,8,64]{0,2,1:T(8,128)}, ...), condition=%wide.region_63.64_spmd.clone, body=%wide.region_61.63_spmd.clone.sunk | while | flops 2724983808 | bytes 207702432 | solution.py:145
  1037.6 10.8 multiply_reduce_fusion.16
  1080.4 10.8 multiply_reduce_fusion.16
  1129.0 10.9 fusion.382
  1140.0 19.6 reduce-scatter.43.cloned.1.call-done
  1166.3 27.9 %all-gather.38.cloned.1.call-done = bf16[1024,1024]{1,0:T(8,128)(2,1)} async-done(((bf16[512,1024]{1,0:T(8,128)(2,1)}), bf16[1024,1024]{1,0:T(8,128)(2,1)}) %all-gather.38.cloned.1.call-update) | async-done | bytes 2097168 | tf_op jit(solution)/shard_map/all_gather | solution.py:49
  1194.3 12.7 fusion.118
  1217.4 10.1 fusion.141
  1228.8 12.5 fusion.132
  1251.9 12.8 fusion.254
  1264.7 14.1 fusion.143
  1321.8 18.3 all-gather.46.cloned.1.call-done
  1345.0 114.4 %while.115 = (s32[]{:T(128)}, f32[1024,8,64]{0,2,1:T(8,128)}, f32[1024,8,64]{0,2,1:T(8,128)}, bf16[2,512,8,64]{1,3,2,0:T(8,128)(2,1)}, s32[2]{0:T(128)S(1)}, /*i...) while((s32[]{:T(128)}, f32[1024,8,64]{0,2,1:T(8,128)}, ...), condition=%wide.region_72.73_spmd.clone, body=%wide.region_70.72_spmd.clone.sunk | while | flops 2726558208 | bytes 225534288 | solution.py:145
  1349.7 10.2 fusion.588
  1360.0 13.5 multiply_reduce_fusion.17
  1373.4 11.5 multiply_convert_fusion.23
  1416.4 13.5 multiply_reduce_fusion.17
  1429.9 11.5 multiply_convert_fusion.23
  1475.1 114.4 %while.113 = (s32[]{:T(128)}, f32[1024,8,64]{0,2,1:T(8,128)}, f32[1024,8,64]{0,2,1:T(8,128)}, bf16[2,512,8,64]{1,3,2,0:T(8,128)(2,1)}, s32[2]{0:T(128)S(1)}, /*i...) while((s32[]{:T(128)}, f32[1024,8,64]{0,2,1:T(8,128)}, ...), condition=%wide.region_54.55_spmd.clone, body=%wide.region_52.54_spmd.clone.sunk | while | flops 2726558208 | bytes 225534288 | solution.py:145
  1479.4 10.1 fusion.565
  1489.5 13.6 multiply_reduce_fusion.15
  1503.1 11.5 multiply_convert_fusion.21
  1536.2 10.0 fusion.565
  1546.2 13.5 multiply_reduce_fusion.15
  1559.7 11.5 multiply_convert_fusion.21
  1600.2 14.1 fusion.142
  1689.3 82.2 %all-reduce.5.cloned.1.call-done = (f32[2,1024]{1,0:T(2,128)}, f32[2,1024]{1,0:T(2,128)}, f32[2,7,1024]{2,1,0:T(8,128)}, f32[2,7,1024]{2,1,0:T(8,128)}) async-done(((f32[2,1024]{1,0:T(2,128)}, f32[2,1024]{1,0:T(2,128)}, f32[2,7,1024]{2,1,0:T(8,128)}, f32[2,7,1024]{2,1,0:T(8,128)}), (f32[2,1024]{1,0:T(2,128)}, f32[2,1024]{1,0:T(2,128)}, f32[2,7,1024]{2,1,0:T(8,128)}, ...) | async-done | bytes 131088 | tf_op jit(solution)/shard_map/psum | solution.py:317
  1774.6 335.1 %all-reduce.7.cloned.1.call-done = (bf16[2,512,1024]{2,1,0:T(8,128)(2,1)}, bf16[2,1024,2048]{2,1,0:T(8,128)(2,1)}, bf16[2,2048,1024]{2,1,0:T(8,128)(2,1)}) async-done(((bf16[2,512,1024]{2,1,0:T(8,128)(2,1)}, bf16[2,1024,2048]{2,1,0:T(8,128)(2,1)}, bf16[2,2048,1024]{2,1,0:T(8,128)(2,1)}), (bf16[2,512,1024]{2,1,0:T(8,128)(2,1)}, bf16[2,1024,2048]{2,1,0:T(8,128)(2,1)}, ...) | async-done | bytes 18874384 | tf_op jit(solution)/shard_map/psum | solution.py:313
  2113.8 13.1 convert_element_type.372
  2126.8 11.7 convert_element_type.373
  2138.5 457.1 %all-gather.48.cloned.1.call-done = bf16[16,2,1024,1536]{3,2,1,0:T(8,128)(2,1)} async-done(((bf16[1,2,1024,1536]{3,2,1,0:T(8,128)(2,1)}), bf16[16,2,1024,1536]{3,2,1,0:T(8,128)(2,1)}) %all-gather.48.cloned.1.call-update) | async-done | bytes 100663312 | tf_op jit(solution)/shard_map/all_gather | solution.py:309
  2595.6 35.2 %reduce_sum.568 = bf16[2,1024,1536]{2,1,0:T(8,128)(2,1)} reduce(bf16[16,2,1024,1536]{3,2,1,0:T(8,128)(2,1)} %all-gather.48.cloned.1.call-done, bf16[]{:T(256)} %constant.201.clone.1), dimensions={0}, to_apply=%region_76.77 | reduce | flops 47185920 | bytes 106954752 | tf_op jit(solution)/shard_map/reduce_sum | solution.py:309
  2640.2 12.6 copy.105
  (914 shorter events, 787.4 us)
Async XLA Ops:
  7.2 42.9 %all-gather.20.cloned.1.call-start = ((), (), s32[]{:S(2)}) async-start(), calls=%async_computation.16 | async-start | bytes 3145728 | tf_op jit(solution)/shard_map/all_gather | solution.py:35
  12.1 128.3 %copy-start.120 = (f32[1,1024]{1,0:T(1,128)}, f32[1,1024]{1,0:T(1,128)S(1)}, u32[]{:S(2)}) copy-start(f32[1,1024]{1,0:T(1,128)S(1)} %get-tuple-element.1007) | copy-start | bytes 12292
  14.2 124.4 %reduce-scatter.17.cloned.1.call-start = ((), (), s32[]{:S(2)}) async-start(), calls=%async_computation.17 | async-start | bytes 3145728 | tf_op jit(solution)/shard_map/reduce_scatter | solution.py:43
  106.6 68.6 %all-gather.28.cloned.1.call-start = ((), (), s32[]{:S(2)}) async-start(), calls=%async_computation.24 | async-start | bytes 3145728 | tf_op jit(solution)/shard_map/all_gather | solution.py:35
  107.1 34.8 %copy-start.128 = (f32[512]{0:T(512)}, f32[512]{0:T(512)S(1)}, u32[]{:S(2)}) copy-start(f32[512]{0:T(512)S(1)} %broadcast_multiply_fusion.3) | copy-start | bytes 6148
  140.4 34.8 %copy-start.168 = (f32[512]{0:T(512)}, f32[512]{0:T(512)S(1)}, u32[]{:S(2)}) copy-start(f32[512]{0:T(512)S(1)} %get-tuple-element.743) | copy-start | bytes 6148
  140.5 34.7 %copy-start.148 = (f32[512]{0:T(512)}, f32[512]{0:T(512)S(1)}, u32[]{:S(2)}) copy-start(f32[512]{0:T(512)S(1)} %fusion.331) | copy-start | bytes 6148
  141.9 121.6 %reduce-scatter.25.cloned.1.call-start = ((), (), s32[]{:S(2)}) async-start(), calls=%async_computation.25 | async-start | bytes 3145728 | tf_op jit(solution)/shard_map/reduce_scatter | solution.py:43
  228.9 34.6 %copy-start.40 = (bf16[512,1024]{1,0:T(8,128)(2,1)S(1)}, bf16[512,1024]{1,0:T(8,128)(2,1)}, u32[]{:S(2)}) copy-start(bf16[512,1024]{1,0:T(8,128)(2,1)} %reduce-scatter.17.cloned.1.call-done) | copy-start | bytes 3145732
  231.6 70.8 %all-gather.30.cloned.1.call-start = ((), (), s32[]{:S(2)}) async-start(), calls=%async_computation.26 | async-start | bytes 3145728 | tf_op jit(solution)/shard_map/all_gather | solution.py:35
  231.8 35.0 %copy-start.140 = (f32[512]{0:T(512)}, f32[512]{0:T(512)S(1)}, u32[]{:S(2)}) copy-start(f32[512]{0:T(512)S(1)} %broadcast_multiply_fusion.6) | copy-start | bytes 6148
  231.8 35.0 %copy-start.136 = (f32[1,1024]{1,0:T(1,128)S(1)}, f32[1,1024]{1,0:T(1,128)}, u32[]{:S(2)}) copy-start(f32[1,1024]{1,0:T(1,128)} %get-tuple-element.1006) | copy-start | bytes 12292
  231.8 35.0 %copy-start.192 = (f32[1,1024]{1,0:T(1,128)S(1)}, f32[1,1024]{1,0:T(1,128)}, u32[]{:S(2)}) copy-start(f32[1,1024]{1,0:T(1,128)} %get-tuple-element.1008) | copy-start | bytes 12292
  269.0 68.4 %all-gather.22.cloned.1.call-start = ((), (), s32[]{:S(2)}) async-start(), calls=%async_computation.18 | async-start | bytes 3145728 | tf_op jit(solution)/shard_map/all_gather | solution.py:35
  269.6 102.5 %reduce-scatter.27.cloned.1.call-start = ((), (), s32[]{:S(2)}) async-start(), calls=%async_computation.27 | async-start | bytes 3145728 | tf_op jit(solution)/shard_map/reduce_scatter | solution.py:43
  321.7 85.2 %reduce-scatter.19.cloned.1.call-start = ((), (), s32[]{:S(2)}) async-start(), calls=%async_computation.19 | async-start | bytes 3145728 | tf_op jit(solution)/shard_map/reduce_scatter | solution.py:43
  356.6 90.2 %all-gather.32.cloned.1.call-start = ((), (), s32[]{:S(2)}) async-start(), calls=%async_computation.28 | async-start | bytes 3145728 | tf_op jit(solution)/shard_map/all_gather | solution.py:35
  358.7 52.6 %copy-start.122 = (f32[1,1024]{1,0:T(1,128)}, f32[1,1024]{1,0:T(1,128)S(1)}, u32[]{:S(2)}) copy-start(f32[1,1024]{1,0:T(1,128)S(1)} %fusion.317) | copy-start | bytes 12292
  413.5 68.4 %all-gather.24.cloned.1.call-start = ((), (), s32[]{:S(2)}) async-start(), calls=%async_computation.20 | async-start | bytes 3145728 | tf_op jit(solution)/shard_map/all_gather | solution.py:35
  418.1 154.1 %reduce-scatter.21.cloned.1.call-start = ((), (), s32[]{:S(2)}) async-start(), calls=%async_computation.21 | async-start | bytes 3145728 | tf_op jit(solution)/shard_map/reduce_scatter | solution.py:43
  422.0 24.8 copy-start.80
  533.2 69.1 %reduce-scatter.29.cloned.1.call-start = ((), (), s32[]{:S(2)}) async-start(), calls=%async_computation.29 | async-start | bytes 3145728 | tf_op jit(solution)/shard_map/reduce_scatter | solution.py:43
  570.4 67.3 %all-gather.26.cloned.1.call-start = ((), (), s32[]{:S(2)}) async-start(), calls=%async_computation.22 | async-start | bytes 3145728 | tf_op jit(solution)/shard_map/all_gather | solution.py:35
  576.4 26.0 copy-start.27
  576.4 96.4 %all-gather.50.cloned.1.call-start = ((), (), s32[]{:S(2)}) async-start(), calls=%async_computation.47 | async-start | bytes 3145728 | tf_op jit(solution)/shard_map/all_gather | solution.py:49
  579.8 128.1 %all-gather.34.cloned.1.call-start = ((), (), s32[]{:S(2)}) async-start(), calls=%async_computation.30 | async-start | bytes 3145728 | tf_op jit(solution)/shard_map/all_gather | solution.py:35
  580.8 23.4 copy-start.134
  604.2 44.3 %copy-start.176 = (f32[512]{0:T(512)}, f32[512]{0:T(512)S(1)}, u32[]{:S(2)}) copy-start(f32[512]{0:T(512)S(1)} %multiply_reduce_fusion.4) | copy-start | bytes 6148
  604.3 44.3 %copy-start.154 = (f32[512]{0:T(512)}, f32[512]{0:T(512)S(1)}, u32[]{:S(2)}) copy-start(f32[512]{0:T(512)S(1)} %fusion.334) | copy-start | bytes 6148
  606.6 135.8 %reduce-scatter.33.cloned.1.call-start = ((), (), s32[]{:S(2)}) async-start(), calls=%async_computation.32 | async-start | bytes 3145728 | tf_op jit(solution)/shard_map/reduce_scatter | solution.py:53
  695.4 81.0 %reduce-scatter.23.cloned.1.call-start = ((), (), s32[]{:S(2)}) async-start(), calls=%async_computation.23 | async-start | bytes 3145728 | tf_op jit(solution)/shard_map/reduce_scatter | solution.py:43
  706.9 104.1 %all-gather.52.cloned.1.call-start = ((), (), s32[]{:S(2)}) async-start(), calls=%async_computation.48 | async-start | bytes 3145728 | tf_op jit(solution)/shard_map/all_gather | solution.py:49
  707.5 34.9 %copy-start.39 = (f32[512,1024]{1,0:T(8,128)S(1)}, f32[512,1024]{1,0:T(8,128)}, u32[]{:S(2)}) copy-start(f32[512,1024]{1,0:T(8,128)} %copy-done.38) | copy-start | bytes 6291460
  707.5 138.8 %all-gather.36.cloned.1.call-start = ((), (), s32[]{:S(2)}) async-start(), calls=%async_computation.33 | async-start | bytes 3145728 | tf_op jit(solution)/shard_map/all_gather | solution.py:49
  742.4 34.1 %copy-start.66 = (bf16[512,1024]{1,0:T(8,128)(2,1)S(1)}, bf16[512,1024]{1,0:T(8,128)(2,1)}, u32[]{:S(2)}) copy-start(bf16[512,1024]{1,0:T(8,128)(2,1)} %reduce-scatter.33.cloned.1.call-done) | copy-start | bytes 3145732
  782.7 167.0 %reduce-scatter.41.cloned.1.call-start = ((), (), s32[]{:S(2)}) async-start(), calls=%async_computation.39 | async-start | bytes 3145728 | tf_op jit(solution)/shard_map/reduce_scatter | solution.py:53
  833.7 120.3 %reduce-scatter.31.cloned.1.call-start = ((), (), s32[]{:S(2)}) async-start(), calls=%async_computation.31 | async-start | bytes 3145728 | tf_op jit(solution)/shard_map/reduce_scatter | solution.py:43
  844.9 136.9 %reduce-scatter.35.cloned.1.call-start = ((), (), s32[]{:S(2)}) async-start(), calls=%async_computation.34 | async-start | bytes 3145728 | tf_op jit(solution)/shard_map/reduce_scatter | solution.py:53
  949.6 74.8 %all-gather.42.cloned.1.call-start = ((), (), s32[]{:S(2)}) async-start(), calls=%async_computation.40 | async-start | bytes 3145728 | tf_op jit(solution)/shard_map/all_gather | solution.py:49
  953.9 28.0 %copy-start.25 = (f32[512,1024]{1,0:T(8,128)S(1)}, f32[512,1024]{1,0:T(8,128)}, u32[]{:S(2)}) copy-start(f32[512,1024]{1,0:T(8,128)} %get-tuple-element.946) | copy-start | bytes 6291460
  953.9 28.0 %copy-start.125 = (f32[1,1024]{1,0:T(1,128)S(1)}, f32[1,1024]{1,0:T(1,128)}, u32[]{:S(2)}) copy-start(f32[1,1024]{1,0:T(1,128)} %copy-done.124) | copy-start | bytes 12292
  953.9 28.0 %copy-start.133 = (f32[512]{0:T(512)S(1)}, f32[512]{0:T(512)}, u32[]{:S(2)}) copy-start(f32[512]{0:T(512)} %copy-done.132) | copy-start | bytes 6148
  958.7 25.8 copy-start.175
  958.7 25.8 copy-start.159
  958.7 28.7 %copy-start.180 = (f32[512]{0:T(512)}, f32[512]{0:T(512)S(1)}, u32[]{:S(2)}) copy-start(f32[512]{0:T(512)S(1)} %negate_multiply_fusion.3) | copy-start | bytes 6148
  958.8 28.7 %copy-start.179 = (f32[512]{0:T(512)S(1)}, f32[512]{0:T(512)}, u32[]{:S(2)}) copy-start(f32[512]{0:T(512)} %copy-done.178) | copy-start | bytes 6148
  991.2 168.4 %reduce-scatter.43.cloned.1.call-start = ((), (), s32[]{:S(2)}) async-start(), calls=%async_computation.41 | async-start | bytes 3145728 | tf_op jit(solution)/shard_map/reduce_scatter | solution.py:53
  991.2 38.4 %copy-start.8 = (bf16[1024,8,64]{0,2,1:T(8,128)(2,1)S(1)}, bf16[1024,8,64]{0,2,1:T(8,128)(2,1)}, u32[]{:S(2)}) copy-start(bf16[1024,8,64]{0,2,1:T(8,128)(2,1)} %copy-done.7) | copy-start | bytes 3145732
  1127.6 66.7 %all-gather.38.cloned.1.call-start = ((), (), s32[]{:S(2)}) async-start(), calls=%async_computation.35 | async-start | bytes 3145728 | tf_op jit(solution)/shard_map/all_gather | solution.py:49
  1129.0 30.6 %copy-start.28 = (f32[512,1024]{1,0:T(8,128)S(1)}, f32[512,1024]{1,0:T(8,128)}, u32[]{:S(2)}) copy-start(f32[512,1024]{1,0:T(8,128)} %copy-done.26) | copy-start | bytes 6291460
  1129.0 30.6 %copy-start.123 = (f32[1,1024]{1,0:T(1,128)S(1)}, f32[1,1024]{1,0:T(1,128)}, u32[]{:S(2)}) copy-start(f32[1,1024]{1,0:T(1,128)} %copy-done.122) | copy-start | bytes 12292
  1129.0 30.6 %copy-start.131 = (f32[512]{0:T(512)S(1)}, f32[512]{0:T(512)}, u32[]{:S(2)}) copy-start(f32[512]{0:T(512)} %copy-done.130) | copy-start | bytes 6148
  1129.0 99.8 %all-gather.44.cloned.1.call-start = ((), (), s32[]{:S(2)}) async-start(), calls=%async_computation.42 | async-start | bytes 3145728 | tf_op jit(solution)/shard_map/all_gather | solution.py:49
  1140.0 24.0 copy-start.181
  1166.3 123.0 %reduce-scatter.37.cloned.1.call-start = ((), (), s32[]{:S(2)}) async-start(), calls=%async_computation.36 | async-start | bytes 3145728 | tf_op jit(solution)/shard_map/reduce_scatter | solution.py:53
  1217.3 79.6 %reduce-scatter.45.cloned.1.call-start = ((), (), s32[]{:S(2)}) async-start(), calls=%async_computation.43 | async-start | bytes 3145728 | tf_op jit(solution)/shard_map/reduce_scatter | solution.py:53
  1251.6 88.4 %all-gather.46.cloned.1.call-start = ((), (), s32[]{:S(2)}) async-start(), calls=%async_computation.44 | async-start | bytes 3145728 | tf_op jit(solution)/shard_map/all_gather | solution.py:49
  1251.9 29.5 %slice-start = ((s8[8388608]{0:T(1024)(128)(4,1)}), s8[4194304]{0:T(1024)(128)(4,1)S(1)}, s32[]{:S(2)}) async-start(s8[8388608]{0:T(1024)(128)(4,1)} %bitcast.742), calls=%async_computation.51 | async-start | bytes 8388608
  1306.8 163.2 %all-gather.40.cloned.1.call-start = ((), (), s32[]{:S(2)}) async-start(), calls=%async_computation.37 | async-start | bytes 3145728 | tf_op jit(solution)/shard_map/all_gather | solution.py:49
  1321.7 321.1 %reduce-scatter.47.cloned.1.call-start = ((), (), s32[]{:S(2)}) async-start(), calls=%async_computation.45 | async-start | bytes 3145728 | tf_op jit(solution)/shard_map/reduce_scatter | solution.py:53
  1470.0 172.9 %reduce-scatter.39.cloned.1.call-start = ((), (), s32[]{:S(2)}) async-start(), calls=%async_computation.38 | async-start | bytes 3145728 | tf_op jit(solution)/shard_map/reduce_scatter | solution.py:53
  1600.2 171.4 %all-reduce.5.cloned.1.call-start = ((), (), s32[]{:S(2)}) async-start(), calls=%async_computation.49 | async-start | bytes 294912 | tf_op jit(solution)/shard_map/psum | solution.py:317
  1649.7 460.0 %all-reduce.7.cloned.1.call-start = ((), (), s32[]{:S(2)}) async-start(), calls=%async_computation.50 | async-start | bytes 37748736 | tf_op jit(solution)/shard_map/psum | solution.py:313
  1652.9 942.8 %all-gather.48.cloned.1.call-start = ((), (), s32[]{:S(2)}) async-start(), calls=%async_computation.46 | async-start | bytes 106954752 | tf_op jit(solution)/shard_map/all_gather | solution.py:309
  (224 other events, 1218.5 us)
Sparse Core Ops, SparseCore 0:
  14.3 35.8 all-gather.19
  106.7 31.8 reduce-scatter.16
  142.0 33.1 all-gather.27
  231.7 31.8 reduce-scatter.24
  269.2 33.1 all-gather.29
  304.3 33.1 all-gather.21
  340.3 31.8 reduce-scatter.26
  375.0 31.8 reduce-scatter.18
  413.6 33.1 all-gather.31
  448.8 33.1 all-gather.23
  533.3 31.8 reduce-scatter.20
  570.5 31.8 reduce-scatter.28
  604.5 33.1 all-gather.25
  639.6 33.1 all-gather.49
  674.7 33.1 all-gather.33
  710.6 31.8 reduce-scatter.32
  744.6 31.8 reduce-scatter.22
  777.9 33.1 all-gather.51
  813.1 33.1 all-gather.35
  848.4 31.8 reduce-scatter.40
  882.6 31.8 reduce-scatter.30
  949.7 32.0 reduce-scatter.34
  991.3 33.1 all-gather.41
  1127.7 31.8 reduce-scatter.42
  1161.1 33.1 all-gather.37
  1195.7 33.1 all-gather.43
  1230.9 31.8 reduce-scatter.36
  1265.1 31.8 reduce-scatter.44
  1306.9 33.1 all-gather.45
  1341.5 33.1 all-gather.39
  1470.1 31.7 reduce-scatter.46
  1600.3 31.8 reduce-scatter.38
  1649.9 121.6 all-reduce.4
  1776.6 333.0 all-reduce.6
  2111.4 484.2 all-gather.47
